TPU v7x, 32 devices: a whole 2x2x4 slice. The times are simulated.
32 devices in a mesh: row: 8 (over y, x, core), col: 4 (over z).
Axes of the slice: x: 2, y: 2, z: 4, core: 2. Of those that a mesh axis runs over, the one named last changes fastest.
Arguments:
- covariance: float32 [2, 8192, 8192], P(None, 'row', 'col'), as said below
- forcing: float32 [2, 8192, 8192], P(None, 'row', 'col'), as said below
- coupling: float32 [2, 64, 64], replicated, may hold values from -0.5 to 0.5
- vertical: float32 [2, 128, 128], replicated, may hold values from -0.375 to 0.375
- damping: float32 [64, 128], replicated, may hold values from 0.3 to 3
- advection: float32 [64, 128], replicated, may hold values from -2 to 2
Outputs:
- advanced: float32 [2, 8192, 8192], P(None, 'row', 'col')
Inputs may be any that keep to these rules, and one draw needn't show every extreme that they name: The covariance equals its conjugate transpose: the real plane is symmetric, the imaginary plane antisymmetric. The forcing equals its conjugate transpose: the real plane is symmetric, the imaginary plane antisymmetric.
All inputs are finite; a program needn't handle non-finite values.
Results may differ from a plain program's by a relative error of at most 0.000073.
Values sent between devices are 32-bit elements; how exact they have to be, the bound alone decides.
A program may use at most 320 MiB of HBM per device.

v0:
```python
import jax
import jax.numpy as jnp
from jax import lax
from jax.sharding import PartitionSpec as P

step_size = 0.25


def complex_einsum(pattern, factor, values):

    def single(factor_part, value_part):
        return jnp.einsum(pattern, factor_part, value_part, precision=lax.Precision.HIGHEST)

    real_part = single(factor[0], values[0]) - single(factor[1], values[1])
    imag_part = single(factor[0], values[1]) + single(factor[1], values[0])
    return jnp.stack([real_part, imag_part])


def complex_scale(factor, values):
    real_part = factor[0] * values[0] - factor[1] * values[1]
    imag_part = factor[0] * values[1] + factor[1] * values[0]
    return jnp.stack([real_part, imag_part])


def conjugate(values):
    return jnp.stack([values[0], -values[1]])


def left_apply(by_rows, coupling, vertical, rates):
    total = complex_einsum("lm,amj->alj", vertical, by_rows)
    total = total + complex_einsum("ab,blj->alj", coupling, by_rows)
    return total + complex_scale(rates[:, :, :, None], by_rows)


def right_apply(by_cols, coupling, vertical, rates):
    total = complex_einsum("lm,iam->ial", conjugate(vertical), by_cols)
    total = total + complex_einsum("ab,ibl->ial", conjugate(coupling), by_cols)
    return total + complex_scale(conjugate(rates)[:, None], by_cols)


def tendency(block_tile, forcing, coupling, vertical, rates):
    rows_here = block_tile.shape[1]
    cols_here = block_tile.shape[2]
    levels = vertical.shape[1]
    lats_row = rows_here // levels
    lats_col = cols_here // levels
    by_rows = block_tile.reshape(2, lats_row, levels, cols_here)
    regrouped = lax.all_to_all(by_rows, "row", split_axis=3, concat_axis=1, tiled=True)
    applied = left_apply(regrouped, coupling, vertical, rates)
    left_term = lax.all_to_all(applied, "row", split_axis=1, concat_axis=3, tiled=True)
    left_term = left_term.reshape(2, rows_here, cols_here)
    by_cols = block_tile.reshape(2, rows_here, lats_col, levels)
    regrouped_cols = lax.all_to_all(by_cols, "col", split_axis=1, concat_axis=2, tiled=True)
    applied_cols = right_apply(regrouped_cols, coupling, vertical, rates)
    right_term = lax.all_to_all(
        applied_cols, "col", split_axis=2, concat_axis=1, tiled=True
    ).reshape(2, rows_here, cols_here)
    return left_term + right_term + forcing


def shards(covariance, forcing, coupling, vertical, damping, advection):
    rates = jnp.stack([-damping, advection])
    first_rate = tendency(covariance, forcing, coupling, vertical, rates)
    midpoint = covariance + 0.5 * step_size * first_rate
    return covariance + step_size * tendency(midpoint, forcing, coupling, vertical, rates)


def solution(mesh):
    return jax.shard_map(
        shards,
        mesh=mesh,
        in_specs=(P(None, "row", "col"), P(None, "row", "col"), P(), P(), P(), P()),
        out_specs=P(None, "row", "col"),
        check_vma=False,
    )
```

profile of v0, /device:TPU:0, one launch (start us, length us, event | category | flops | bytes accessed | tf_op | source)
XLA Modules:
  0.0 2441.1 jit_solution(17442187832632348149)
XLA Ops:
  0.0 17.6 copy.149
  39.9 168.1 %all-to-all-done = f32[2,8,128,2048]{2,1,0,3:T(8,128)} async-done(((f32[2,8,128,2048]{2,1,0,3:T(8,128)}), f32[2,8,128,2048]{2,1,0,3:T(8,128)}, u32[]{:S(2)}, u32[]{:S(2)}) %all-to-all-start) | async-done | bytes 16777248 | tf_op jit(solution)/shard_map/all_to_all | solution.py:48
  247.9 11.7 fusion.90
  285.8 11.9 fusion.78
  307.0 11.8 fusion.88
  328.0 12.0 fusion.76
  349.3 11.0 fusion.46
  397.3 19.0 add_bitcast_fusion.4
  416.3 16.7 fusion
  439.1 137.1 %all-to-all-done.2 = f32[2,1024,16,128]{3,2,0,1:T(8,128)} async-done(((f32[2,1024,16,128]{3,2,0,1:T(8,128)}), f32[2,1024,16,128]{3,2,0,1:T(8,128)}, u32[]{:S(2)}, u32[]{:S(2)}) %all-to-all-start.2) | async-done | bytes 16777248 | tf_op jit(solution)/shard_map/all_to_all | solution.py:53
  607.0 17.1 fusion.16
  624.1 17.2 fusion.18
  641.2 17.4 fusion.20
  658.6 17.1 fusion.22
  693.1 10.9 add_bitcast_fusion.3
  720.1 41.0 %fusion.6 = (f32[1,256,64,128]{3,1,2,0:T(8,128)}, f32[1,256,64,128]{3,1,2,0:T(8,128)}) fusion(f32[256,128,64]{1,2,0:T(8,128)} %fusion.20, f32[256,128,64]{1,2,0:T(8,128)} %fusion.16, f32[256,128,64]{1,2,0:T(8,128)} %fusion.18, f32[256,128,64]{1,2,0:T(8,128)} %fusion.22), kind=kLoop, calls=%fused_computation.16 | loop fusion | flops 4194304 | bytes 50331648 | tf_op jit(solution)/shard_map/stack | solution.py:16
  761.2 16.7 fusion.1
  791.0 17.4 copy.164
  808.4 18.0 reshape.251
  826.3 328.4 %all-to-all-done.3 = f32[2,256,64,128]{3,1,0,2:T(8,128)} async-done(((f32[2,256,64,128]{3,1,0,2:T(8,128)}), f32[2,256,64,128]{3,1,0,2:T(8,128)}, u32[]{:S(2)}, u32[]{:S(2)}) %all-to-all-start.3) | async-done | bytes 16777248 | tf_op jit(solution)/shard_map/all_to_all | solution.py:55
  1154.7 17.8 copy.249
  1172.5 18.0 reshape.253
  1190.4 29.2 %multiply_add_fusion.1 = f32[2,1024,2048]{2,1,0:T(8,128)} fusion(f32[2,1024,2048]{2,1,0:T(8,128)} %param.6, f32[2,1024,2048]{2,1,0:T(8,128)} %param.7, f32[2,1024,2048]{2,1,0:T(8,128)} %reshape.251, f32[2,1024,2048]{2,1,0:T(8,128)} %reshape.253), kind=kLoop, calls=%fused_computation.10 | loop fusion | flops 16777216 | bytes 83886080 | tf_op jit(solution)/shard_map/add | solution.py:64
  1219.6 17.7 copy.181
  1259.5 167.4 %all-to-all-done.4 = f32[2,8,128,2048]{2,1,0,3:T(8,128)} async-done(((f32[2,8,128,2048]{2,1,0,3:T(8,128)}), f32[2,8,128,2048]{2,1,0,3:T(8,128)}, u32[]{:S(2)}, u32[]{:S(2)}) %all-to-all-start.4) | async-done | bytes 16777248 | tf_op jit(solution)/shard_map/all_to_all | solution.py:48
  1470.9 11.9 fusion.84
  1501.2 12.1 fusion.74
  1522.6 11.9 fusion.82
  1543.7 12.3 fusion.72
  1602.4 11.2 subtract_bitcast_fusion.1
  1613.6 11.3 add_bitcast_fusion.1
  1624.9 11.2 multiply_subtract_fusion.1
  1636.1 16.7 fusion.2
  1659.0 135.3 %all-to-all-done.6 = f32[2,1024,16,128]{3,2,0,1:T(8,128)} async-done(((f32[2,1024,16,128]{3,2,0,1:T(8,128)}), f32[2,1024,16,128]{3,2,0,1:T(8,128)}, u32[]{:S(2)}, u32[]{:S(2)}) %all-to-all-start.6) | async-done | bytes 16777248 | tf_op jit(solution)/shard_map/all_to_all | solution.py:53
  1828.1 17.2 fusion.14
  1845.3 17.4 fusion.12
  1862.7 17.0 fusion.10
  1879.7 17.1 fusion.8
  1934.3 18.2 fusion.5
  1952.6 18.4 fusion.4
  1970.9 11.2 multiply_subtract_fusion
  1982.2 16.7 fusion.3
  2012.2 17.4 copy.196
  2029.6 18.0 reshape.255
  2047.5 328.4 %all-to-all-done.7 = f32[2,256,64,128]{3,1,0,2:T(8,128)} async-done(((f32[2,256,64,128]{3,1,0,2:T(8,128)}), f32[2,256,64,128]{3,1,0,2:T(8,128)}, u32[]{:S(2)}, u32[]{:S(2)}) %all-to-all-start.7) | async-done | bytes 16777248 | tf_op jit(solution)/shard_map/all_to_all | solution.py:55
  2375.9 17.8 copy.212
  2393.7 18.0 reshape.257
  2411.7 29.2 %multiply_add_fusion = f32[2,1024,2048]{2,1,0:T(8,128)} fusion(f32[2,1024,2048]{2,1,0:T(8,128)} %param.6, f32[2,1024,2048]{2,1,0:T(8,128)} %param.7, f32[2,1024,2048]{2,1,0:T(8,128)} %reshape.255, f32[2,1024,2048]{2,1,0:T(8,128)} %reshape.257), kind=kLoop, calls=%fused_computation.9 | loop fusion | flops 16777216 | bytes 83886080 | tf_op jit(solution)/shard_map/add | solution.py:65
  (112 shorter events, 476.8 us)
Async XLA Ops:
  17.6 190.4 %all-to-all-start = ((f32[2,8,128,2048]{2,1,0,3:T(8,128)}), f32[2,8,128,2048]{2,1,0,3:T(8,128)}, u32[]{:S(2)}, u32[]{:S(2)}) async-start(f32[2,8,128,2048]{2,1,0,3:T(8,128)} %copy.149), calls=%async_computation | async-start | bytes 33554432 | tf_op jit(solution)/shard_map/all_to_all | solution.py:48
  39.9 175.3 %copy-start.13 = (f32[64,128]{1,0:T(8,128)S(1)}, f32[64,128]{1,0:T(8,128)}, u32[]{:S(2)}) copy-start(f32[64,128]{1,0:T(8,128)} %param.10) | copy-start | bytes 98308
  208.0 368.2 %all-to-all-start.2 = ((f32[2,1024,16,128]{3,2,0,1:T(8,128)}), f32[2,1024,16,128]{3,2,0,1:T(8,128)}, u32[]{:S(2)}, u32[]{:S(2)}) async-start(f32[2,1024,16,128]{3,2,0,1:T(8,128)} %copy.213), calls=%async_computation.2 | async-start | bytes 33554432 | tf_op jit(solution)/shard_map/all_to_all | solution.py:53
  215.2 497.9 %copy-start.7 = (f32[64,128]{1,0:T(8,128)}, f32[64,128]{1,0:T(8,128)S(1)}, u32[]{:S(2)}) copy-start(f32[64,128]{1,0:T(8,128)S(1)} %neg.27) | copy-start | bytes 98308
  238.7 9.2 copy-start.5
  340.0 9.3 copy-start.3
  349.3 20.4 slice-start.6
  349.3 31.2 %slice-start.4 = ((s8[8388608]{0:T(1024)(128)(4,1)}), s8[4194304]{0:T(1024)(128)(4,1)S(1)}, s32[]{:S(2)}) async-start(s8[8388608]{0:T(1024)(128)(4,1)} %bitcast.244), calls=%async_computation.12 | async-start | bytes 8388608
  360.4 9.3 slice-start.7
  360.4 20.2 slice-start.5
  380.6 9.6 copy-start.9
  576.2 207.7 %all-to-all-start.1 = ((f32[2,64,128,256]{2,3,0,1:T(8,128)}), f32[2,64,128,256]{2,3,0,1:T(8,128)}, u32[]{:S(2)}, u32[]{:S(2)}) async-start(f32[2,64,128,256]{2,3,0,1:T(8,128)} %copy.163), calls=%async_computation.1 | async-start | bytes 33554432 | tf_op jit(solution)/shard_map/all_to_all | solution.py:50
  582.2 130.9 %copy-start.11 = (f32[64,128]{1,0:T(8,128)}, f32[64,128]{1,0:T(8,128)S(1)}, u32[]{:S(2)}) copy-start(f32[64,128]{1,0:T(8,128)S(1)} %neg.32) | copy-start | bytes 98308
  784.0 370.8 %all-to-all-start.3 = ((f32[2,256,64,128]{3,1,0,2:T(8,128)}), f32[2,256,64,128]{3,1,0,2:T(8,128)}, u32[]{:S(2)}, u32[]{:S(2)}) async-start(f32[2,256,64,128]{3,1,0,2:T(8,128)} %copy.179), calls=%async_computation.3 | async-start | bytes 33554432 | tf_op jit(solution)/shard_map/all_to_all | solution.py:55
  1237.3 189.7 %all-to-all-start.4 = ((f32[2,8,128,2048]{2,1,0,3:T(8,128)}), f32[2,8,128,2048]{2,1,0,3:T(8,128)}, u32[]{:S(2)}, u32[]{:S(2)}) async-start(f32[2,8,128,2048]{2,1,0,3:T(8,128)} %copy.181), calls=%async_computation.4 | async-start | bytes 33554432 | tf_op jit(solution)/shard_map/all_to_all | solution.py:48
  1426.9 367.4 %all-to-all-start.6 = ((f32[2,1024,16,128]{3,2,0,1:T(8,128)}), f32[2,1024,16,128]{3,2,0,1:T(8,128)}, u32[]{:S(2)}, u32[]{:S(2)}) async-start(f32[2,1024,16,128]{3,2,0,1:T(8,128)} %copy.197), calls=%async_computation.6 | async-start | bytes 33554432 | tf_op jit(solution)/shard_map/all_to_all | solution.py:53
  1450.0 7.8 copy-start.2
  1461.7 9.2 copy-start.6
  1556.0 9.3 copy-start.4
  1565.3 18.7 slice-start.2
  1565.3 27.8 %slice-start = ((s8[8388608]{0:T(1024)(128)(4,1)}), s8[4194304]{0:T(1024)(128)(4,1)S(1)}, s32[]{:S(2)}) async-start(s8[8388608]{0:T(1024)(128)(4,1)} %bitcast.233), calls=%async_computation.8 | async-start | bytes 8388608
  1574.7 9.4 slice-start.3
  1574.7 18.5 slice-start.1
  1613.6 11.3 copy-start.8
  1613.6 11.3 copy-start.10
  1794.3 210.6 %all-to-all-start.5 = ((f32[2,64,128,256]{2,3,0,1:T(8,128)}), f32[2,64,128,256]{2,3,0,1:T(8,128)}, u32[]{:S(2)}, u32[]{:S(2)}) async-start(f32[2,64,128,256]{2,3,0,1:T(8,128)} %copy.195), calls=%async_computation.5 | async-start | bytes 33554432 | tf_op jit(solution)/shard_map/all_to_all | solution.py:50
  1819.1 106.0 %copy-start = (f32[1,256,4,16,128]{4,1,3,2,0:T(8,128)}, f32[1,256,4,16,128]{4,1,3,2,0:T(8,128)S(1)}, u32[]{:S(2)}) copy-start(f32[1,256,4,16,128]{4,1,3,2,0:T(8,128)S(1)} %copy.199) | copy-start | bytes 25165828
  1828.1 86.1 %copy-start.1 = (f32[1,256,4,16,128]{4,1,3,2,0:T(8,128)}, f32[1,256,4,16,128]{4,1,3,2,0:T(8,128)S(1)}, u32[]{:S(2)}) copy-start(f32[1,256,4,16,128]{4,1,3,2,0:T(8,128)S(1)} %copy.200) | copy-start | bytes 25165828
  1952.6 18.4 copy-start.12
  2004.9 371.0 %all-to-all-start.7 = ((f32[2,256,64,128]{3,1,0,2:T(8,128)}), f32[2,256,64,128]{3,1,0,2:T(8,128)}, u32[]{:S(2)}, u32[]{:S(2)}) async-start(f32[2,256,64,128]{3,1,0,2:T(8,128)} %copy.211), calls=%async_computation.7 | async-start | bytes 33554432 | tf_op jit(solution)/shard_map/all_to_all | solution.py:55
where the time goes:
time: 2450 us; the launch traced here: 2440 us
  waiting for transfers between devices  1260 us (51%)
  local copies, waits for them, and re-layouts  457 us (19%)
  matrix products  386 us (16%)
  other arithmetic  281 us (11%)
  starting transfers between devices  52 us (2%)
    all_to_all x2, waiting for transfers between devices, tendency(): lax.all_to_all(applied_cols, 'col', split_axis=2, concat_axis=1, tiled=True)  657 us
    dot_general x32, matrix products, single(): jnp.einsum(pattern, factor_part, value_part, precision=lax.Precision.HIGH...  386 us
    all_to_all x2, waiting for transfers between devices, tendency(): lax.all_to_all(by_rows, 'row', split_axis=3, concat_axis=1, tiled=True)  336 us
    all_to_all x2, waiting for transfers between devices, tendency(): lax.all_to_all(by_cols, 'col', split_axis=1, concat_axis=2, tiled=True)  272 us
    another operation x6, other arithmetic, complex_einsum(): return jnp.stack([real_part, imag_part])  119 us
    slice x12, local copies, waits for them, and re-layouts, complex_einsum(): real_part = single(factor[0], values[0]) - single(factor[1], values[1])  79.4 us
    dot_general x8, local copies, waits for them, and re-layouts, single(): jnp.einsum(pattern, factor_part, value_part, precision=lax.Precision.HIGH...  74.2 us
  transfers between devices with their start and end apart: 8, of which 6 were waited for; matrix products, arithmetic and copies ran while one was open for 39% of the time, Pallas kernels for 0%

commit v1 on v0

--- a/solution.py
+++ b/solution.py
@@ -4,6 +4,29 @@
 from jax.sharding import PartitionSpec as P
 
 step_size = 0.25
+
+
+def in_blocks(value, dim, length):
+    lengths = value.shape
+    parts = value.reshape(*lengths[:dim], length, lengths[dim] // length, *lengths[dim + 1 :])
+    return jnp.moveaxis(parts, dim, 0)
+
+
+def joined_along(blocks, dim):
+    dims = list(blocks.shape[1:])
+    dims[dim] *= blocks.shape[0]
+    return jnp.moveaxis(blocks, 0, dim).reshape(dims)
+
+
+def rotated_exchange(shard, axis, split_dim, concat_dim):
+    size, index = (lax.axis_size(axis), lax.axis_index(axis))
+    blocks = in_blocks(shard, split_dim, size)
+    outs = [blocks[index]]
+    for step in range(1, size):
+        sent = blocks[(index + step) % size]
+        outs.append(lax.ppermute(sent, axis, [(i, (i + step) % size) for i in range(size)]))
+    blocks = jnp.stack(outs)[(index - jnp.arange(size)) % size]
+    return joined_along(blocks, concat_dim)
 
 
 def complex_einsum(pattern, factor, values):
@@ -50,7 +73,7 @@
     left_term = lax.all_to_all(applied, "row", split_axis=1, concat_axis=3, tiled=True)
     left_term = left_term.reshape(2, rows_here, cols_here)
     by_cols = block_tile.reshape(2, rows_here, lats_col, levels)
-    regrouped_cols = lax.all_to_all(by_cols, "col", split_axis=1, concat_axis=2, tiled=True)
+    regrouped_cols = rotated_exchange(by_cols, "col", 1, 2)
     applied_cols = right_apply(regrouped_cols, coupling, vertical, rates)
     right_term = lax.all_to_all(
         applied_cols, "col", split_axis=2, concat_axis=1, tiled=True

time: 2450 us -> 2480 us (1.012)
  waiting for transfers between devices: 1260 us -> 1070 us
  starting transfers between devices: 52 us -> 219 us
  local copies, waits for them, and re-layouts: 457 us -> 497 us
  other arithmetic: 281 us -> 306 us
    ppermute x0 -> x6, waiting for transfers between devices: none -> 489 us  [rotated_exchange(): lax.ppermute(sent, axis, [(i, (i + step) % size) for i in range(size)])]
    all_to_all x2, waiting for transfers between devices: 657 us -> 280 us  [tendency(): lax.all_to_all(applied_cols, 'col', split_axis=2, concat_axis=1, tiled=True)]
    all_to_all x2, waiting for transfers between devices: 336 us -> 0.01 us  [tendency(): lax.all_to_all(by_rows, 'row', split_axis=3, concat_axis=1, tiled=True)]
    all_to_all x2, waiting for transfers between devices: 0.01 us -> 297 us  [tendency(): lax.all_to_all(applied, 'row', split_axis=1, concat_axis=3, tiled=True)]
    all_to_all x2 -> x0, waiting for transfers between devices: 272 us -> none  [tendency(): lax.all_to_all(by_cols, 'col', split_axis=1, concat_axis=2, tiled=True)]
    all_to_all x2, starting transfers between devices: 14.3 us -> 184 us  [tendency(): lax.all_to_all(applied_cols, 'col', split_axis=2, concat_axis=1, tiled=True)]
    gather x0 -> x6, local copies, waits for them, and re-layouts: none -> 44.1 us  [rotated_exchange(): blocks = jnp.stack(outs)[(index - jnp.arange(size)) % size]]
  transfers between devices with their start and end apart: 8 -> 12, of which waited for: 6 -> 8; matrix products, arithmetic and copies ran while one was open for 39% -> 41% of each run, Pallas kernels for 0% -> 0%
where the time goes in v1:
time: 2480 us
  waiting for transfers between devices  1070 us (43%)
  local copies, waits for them, and re-layouts  497 us (20%)
  matrix products  386 us (16%)
  other arithmetic  306 us (12%)
  starting transfers between devices  219 us (9%)
    ppermute x6, waiting for transfers between devices, rotated_exchange(): lax.ppermute(sent, axis, [(i, (i + step) % size) for i in range(size)])  489 us
    dot_general x32, matrix products, single(): jnp.einsum(pattern, factor_part, value_part, precision=lax.Precision.HIGH...  386 us
    all_to_all x2, waiting for transfers between devices, tendency(): lax.all_to_all(applied, 'row', split_axis=1, concat_axis=3, tiled=True)  297 us
    all_to_all x2, waiting for transfers between devices, tendency(): lax.all_to_all(applied_cols, 'col', split_axis=2, concat_axis=1, tiled=True)  280 us
    all_to_all x2, starting transfers between devices, tendency(): lax.all_to_all(applied_cols, 'col', split_axis=2, concat_axis=1, tiled=True)  184 us
    another operation x6, other arithmetic, complex_einsum(): return jnp.stack([real_part, imag_part])  119 us
    slice x12, local copies, waits for them, and re-layouts, complex_einsum(): real_part = single(factor[0], values[0]) - single(factor[1], values[1])  79.6 us
    dot_general x8, local copies, waits for them, and re-layouts, single(): jnp.einsum(pattern, factor_part, value_part, precision=lax.Precision.HIGH...  74.2 us
  transfers between devices with their start and end apart: 12, of which 8 were waited for; matrix products, arithmetic and copies ran while one was open for 41% of the time, Pallas kernels for 0%

profile of v1, /device:TPU:0, one launch (start us, length us, event | category | flops | bytes accessed | tf_op | source)
XLA Modules:
  0.0 2475.2 jit_solution(8303265567410762608)
XLA Ops:
  0.0 14.2 copy.241
  14.2 12.2 dynamic-slice_bitcast_fusion.7
  33.3 17.6 copy.165
  57.1 66.2 %collective-permute-done = f32[2,256,16,128]{3,2,1,0:T(8,128)} collective-permute-done((f32[2,256,16,128]{3,2,1,0:T(8,128)}, f32[2,256,16,128]{3,2,1,0:T(8,128)}, u32[]{:S(2)}, u32[]{:S(2)}) %collective-permute-start) | collective-permute-done | bytes 4194336 | tf_op jit(solution)/shard_map/ppermute | solution.py:27
  123.3 178.9 %collective-permute-done.1 = f32[2,256,16,128]{3,2,1,0:T(8,128)} collective-permute-done((f32[2,256,16,128]{3,2,1,0:T(8,128)}, f32[2,256,16,128]{3,2,1,0:T(8,128)}, u32[]{:S(2)}, u32[]{:S(2)}) %collective-permute-start.1) | collective-permute-done | bytes 4194336 | tf_op jit(solution)/shard_map/ppermute | solution.py:27
  355.2 17.1 fusion.16
  372.3 17.1 fusion.18
  389.4 17.4 fusion.20
  406.8 17.0 fusion.22
  468.5 40.8 %fusion.6 = (f32[1,256,64,128]{3,1,2,0:T(8,128)}, f32[1,256,64,128]{3,1,2,0:T(8,128)}) fusion(f32[256,128,64]{1,2,0:T(8,128)} %fusion.20, f32[256,128,64]{1,2,0:T(8,128)} %fusion.16, f32[256,128,64]{1,2,0:T(8,128)} %fusion.18, f32[256,128,64]{1,2,0:T(8,128)} %fusion.22), kind=kLoop, calls=%fused_computation.24 | loop fusion | flops 4194304 | bytes 50331648 | tf_op jit(solution)/shard_map/stack | solution.py:39
  509.3 16.7 fusion.1
  532.1 92.6 %all-to-all-start.2 = ((f32[2,256,64,128]{3,1,0,2:T(8,128)}), f32[2,256,64,128]{3,1,0,2:T(8,128)}, u32[]{:S(2)}, u32[]{:S(2)}) async-start(f32[2,256,64,128]{3,1,0,2:T(8,128)} %copy.197), calls=%async_computation.2 | async-start | bytes 33554432 | tf_op jit(solution)/shard_map/all_to_all | solution.py:78
  657.4 11.7 fusion.90
  695.4 12.2 fusion.78
  716.8 11.8 fusion.88
  737.9 11.9 fusion.76
  806.6 18.9 add_bitcast_fusion.4
  825.6 16.7 fusion
  848.5 140.7 %all-to-all-done.2 = f32[2,256,64,128]{3,1,0,2:T(8,128)} async-done(((f32[2,256,64,128]{3,1,0,2:T(8,128)}), f32[2,256,64,128]{3,1,0,2:T(8,128)}, u32[]{:S(2)}, u32[]{:S(2)}) %all-to-all-start.2) | async-done | bytes 16777248 | tf_op jit(solution)/shard_map/all_to_all | solution.py:78
  995.3 17.7 copy.276
  1013.1 18.0 reshape.311
  1031.0 148.2 %all-to-all-done.1 = f32[2,64,128,256]{2,3,0,1:T(8,128)} async-done(((f32[2,64,128,256]{2,3,0,1:T(8,128)}), f32[2,64,128,256]{2,3,0,1:T(8,128)}, u32[]{:S(2)}, u32[]{:S(2)}) %all-to-all-start.1) | async-done | bytes 16777248 | tf_op jit(solution)/shard_map/all_to_all | solution.py:73
  1179.3 17.4 copy.180
  1196.6 18.0 reshape.310
  1214.6 29.2 %multiply_add_fusion.1 = f32[2,1024,2048]{2,1,0:T(8,128)} fusion(f32[2,1024,2048]{2,1,0:T(8,128)} %param.6, f32[2,1024,2048]{2,1,0:T(8,128)} %param.7, f32[2,1024,2048]{2,1,0:T(8,128)} %reshape.310, f32[2,1024,2048]{2,1,0:T(8,128)} %reshape.311), kind=kLoop, calls=%fused_computation.18 | loop fusion | flops 16777216 | bytes 83886080 | tf_op jit(solution)/shard_map/add | solution.py:87
  1263.0 17.7 copy.199
  1286.6 68.1 %collective-permute-done.3 = f32[2,256,16,128]{3,2,1,0:T(8,128)} collective-permute-done((f32[2,256,16,128]{3,2,1,0:T(8,128)}, f32[2,256,16,128]{3,2,1,0:T(8,128)}, u32[]{:S(2)}, u32[]{:S(2)}) %collective-permute-start.3) | collective-permute-done | bytes 4194336 | tf_op jit(solution)/shard_map/ppermute | solution.py:27
  1354.7 175.7 %collective-permute-done.4 = f32[2,256,16,128]{3,2,1,0:T(8,128)} collective-permute-done((f32[2,256,16,128]{3,2,1,0:T(8,128)}, f32[2,256,16,128]{3,2,1,0:T(8,128)}, u32[]{:S(2)}, u32[]{:S(2)}) %collective-permute-start.4) | collective-permute-done | bytes 4194336 | tf_op jit(solution)/shard_map/ppermute | solution.py:27
  1587.1 17.2 fusion.14
  1604.3 17.1 fusion.12
  1621.4 17.3 fusion.10
  1638.8 17.1 fusion.8
  1693.5 18.2 fusion.5
  1711.7 18.4 fusion.4
  1741.2 16.7 fusion.3
  1764.0 91.8 %all-to-all-start.5 = ((f32[2,256,64,128]{3,1,0,2:T(8,128)}), f32[2,256,64,128]{3,1,0,2:T(8,128)}, u32[]{:S(2)}, u32[]{:S(2)}) async-start(f32[2,256,64,128]{3,1,0,2:T(8,128)} %copy.231), calls=%async_computation.5 | async-start | bytes 33554432 | tf_op jit(solution)/shard_map/all_to_all | solution.py:78
  1892.6 11.9 fusion.84
  1923.0 12.3 fusion.74
  1944.7 12.0 fusion.82
  1965.9 12.0 fusion.72
  2058.0 16.7 fusion.2
  2080.9 138.8 %all-to-all-done.5 = f32[2,256,64,128]{3,1,0,2:T(8,128)} async-done(((f32[2,256,64,128]{3,1,0,2:T(8,128)}), f32[2,256,64,128]{3,1,0,2:T(8,128)}, u32[]{:S(2)}, u32[]{:S(2)}) %all-to-all-start.5) | async-done | bytes 16777248 | tf_op jit(solution)/shard_map/all_to_all | solution.py:78
  2225.8 17.7 copy.232
  2243.5 18.0 reshape.314
  2261.4 149.0 %all-to-all-done.4 = f32[2,64,128,256]{2,3,0,1:T(8,128)} async-done(((f32[2,64,128,256]{2,3,0,1:T(8,128)}), f32[2,64,128,256]{2,3,0,1:T(8,128)}, u32[]{:S(2)}, u32[]{:S(2)}) %all-to-all-start.4) | async-done | bytes 16777248 | tf_op jit(solution)/shard_map/all_to_all | solution.py:73
  2410.4 17.4 copy.214
  2427.8 18.0 reshape.313
  2445.8 29.2 %multiply_add_fusion = f32[2,1024,2048]{2,1,0:T(8,128)} fusion(f32[2,1024,2048]{2,1,0:T(8,128)} %param.6, f32[2,1024,2048]{2,1,0:T(8,128)} %param.7, f32[2,1024,2048]{2,1,0:T(8,128)} %reshape.313, f32[2,1024,2048]{2,1,0:T(8,128)} %reshape.314), kind=kLoop, calls=%fused_computation.17 | loop fusion | flops 16777216 | bytes 83886080 | tf_op jit(solution)/shard_map/add | solution.py:88
  (138 shorter events, 566.1 us)
Async XLA Ops:
  26.3 97.0 %collective-permute-start = (f32[2,256,16,128]{3,2,1,0:T(8,128)}, f32[2,256,16,128]{3,2,1,0:T(8,128)}, u32[]{:S(2)}, u32[]{:S(2)}) collective-permute-start(f32[2,256,16,128]{3,2,1,0:T(8,128)} %get-tuple-element.29), channel_id=1, source_target_pairs={{0,1},{1,2},{2,3},{3,0},{4,5},{5,6},{6,7},{7,4},{8,9},{9,10},{10,1... | collective-permute-start | bytes 12582920 | tf_op jit(solution)/shard_map/ppermute | solution.py:27
  29.4 272.8 %collective-permute-start.1 = (f32[2,256,16,128]{3,2,1,0:T(8,128)}, f32[2,256,16,128]{3,2,1,0:T(8,128)}, u32[]{:S(2)}, u32[]{:S(2)}) collective-permute-start(f32[2,256,16,128]{3,2,1,0:T(8,128)} %get-tuple-element.28), channel_id=1, source_target_pairs={{0,2},{1,3},{2,0},{3,1},{4,6},{5,7},{6,4},{7,5},{8,10},{9,11},{10,... | collective-permute-start | bytes 12582920 | tf_op jit(solution)/shard_map/ppermute | solution.py:27
  32.0 270.2 %collective-permute-start.2 = (f32[2,256,16,128]{3,2,1,0:T(8,128)}, f32[2,256,16,128]{3,2,1,0:T(8,128)}, u32[]{:S(2)}, u32[]{:S(2)}) collective-permute-start(f32[2,256,16,128]{3,2,1,0:T(8,128)} %get-tuple-element.30), channel_id=1, source_target_pairs={{0,3},{1,0},{2,1},{3,2},{4,7},{5,4},{6,5},{7,6},{8,11},{9,8},{10,9... | collective-permute-start | bytes 12582920 | tf_op jit(solution)/shard_map/ppermute | solution.py:27
  51.0 6.1 copy-start.16
  51.0 6.1 copy-start.11
  51.0 481.1 %all-to-all-start = ((f32[2,8,128,2048]{2,1,0,3:T(8,128)}), f32[2,8,128,2048]{2,1,0,3:T(8,128)}, u32[]{:S(2)}, u32[]{:S(2)}) async-start(f32[2,8,128,2048]{2,1,0,3:T(8,128)} %copy.165), calls=%async_computation | async-start | bytes 33554432 | tf_op jit(solution)/shard_map/all_to_all | solution.py:71
  57.1 404.3 %copy-start.7 = (f32[64,128]{1,0:T(8,128)}, f32[64,128]{1,0:T(8,128)S(1)}, u32[]{:S(2)}) copy-start(f32[64,128]{1,0:T(8,128)S(1)} %neg.27) | copy-start | bytes 98308
  57.1 404.3 %copy-start.14 = (f32[64,128]{1,0:T(8,128)}, f32[64,128]{1,0:T(8,128)S(1)}, u32[]{:S(2)}) copy-start(f32[64,128]{1,0:T(8,128)S(1)} %neg.32) | copy-start | bytes 98308
  57.1 265.6 %copy-start.17 = (s32[1024]{0:T(1024)}, s32[1024]{0:T(1024)S(1)}, u32[]{:S(2)}) copy-start(s32[1024]{0:T(1024)S(1)} %pad_clamp_fusion) | copy-start | bytes 12292
  349.2 6.0 copy-start.5
  406.8 17.0 copy-start.3
  532.1 457.1 %all-to-all-start.2 = ((f32[2,256,64,128]{3,1,0,2:T(8,128)}), f32[2,256,64,128]{3,1,0,2:T(8,128)}, u32[]{:S(2)}, u32[]{:S(2)}) async-start(f32[2,256,64,128]{3,1,0,2:T(8,128)} %copy.197), calls=%async_computation.2 | async-start | bytes 33554432 | tf_op jit(solution)/shard_map/all_to_all | solution.py:78
  759.1 20.3 slice-start.6
  759.1 31.2 %slice-start.4 = ((s8[8388608]{0:T(1024)(128)(4,1)}), s8[4194304]{0:T(1024)(128)(4,1)S(1)}, s32[]{:S(2)}) async-start(s8[8388608]{0:T(1024)(128)(4,1)} %bitcast.282), calls=%async_computation.10 | async-start | bytes 8388608
  770.1 9.3 slice-start.7
  770.1 20.2 slice-start.5
  790.3 9.4 copy-start.8
  790.3 9.4 copy-start.12
  989.2 190.1 %all-to-all-start.1 = ((f32[2,64,128,256]{2,3,0,1:T(8,128)}), f32[2,64,128,256]{2,3,0,1:T(8,128)}, u32[]{:S(2)}, u32[]{:S(2)}) async-start(f32[2,64,128,256]{2,3,0,1:T(8,128)} %copy.179), calls=%async_computation.1 | async-start | bytes 33554432 | tf_op jit(solution)/shard_map/all_to_all | solution.py:73
  1259.1 95.6 %collective-permute-start.3 = (f32[2,256,16,128]{3,2,1,0:T(8,128)}, f32[2,256,16,128]{3,2,1,0:T(8,128)}, u32[]{:S(2)}, u32[]{:S(2)}) collective-permute-start(f32[2,256,16,128]{3,2,1,0:T(8,128)} %get-tuple-element.19), channel_id=1, source_target_pairs={{0,1},{1,2},{2,3},{3,0},{4,5},{5,6},{6,7},{7,4},{8,9},{9,10},{10,1... | collective-permute-start | bytes 12582920 | tf_op jit(solution)/shard_map/ppermute | solution.py:27
  1259.6 270.9 %collective-permute-start.4 = (f32[2,256,16,128]{3,2,1,0:T(8,128)}, f32[2,256,16,128]{3,2,1,0:T(8,128)}, u32[]{:S(2)}, u32[]{:S(2)}) collective-permute-start(f32[2,256,16,128]{3,2,1,0:T(8,128)} %get-tuple-element.18), channel_id=1, source_target_pairs={{0,2},{1,3},{2,0},{3,1},{4,6},{5,7},{6,4},{7,5},{8,10},{9,11},{10,... | collective-permute-start | bytes 12582920 | tf_op jit(solution)/shard_map/ppermute | solution.py:27
  1263.0 267.5 %collective-permute-start.5 = (f32[2,256,16,128]{3,2,1,0:T(8,128)}, f32[2,256,16,128]{3,2,1,0:T(8,128)}, u32[]{:S(2)}, u32[]{:S(2)}) collective-permute-start(f32[2,256,16,128]{3,2,1,0:T(8,128)} %get-tuple-element.20), channel_id=1, source_target_pairs={{0,3},{1,0},{2,1},{3,2},{4,7},{5,4},{6,5},{7,6},{8,11},{9,8},{10,9... | collective-permute-start | bytes 12582920 | tf_op jit(solution)/shard_map/ppermute | solution.py:27
  1280.7 483.3 %all-to-all-start.3 = ((f32[2,8,128,2048]{2,1,0,3:T(8,128)}), f32[2,8,128,2048]{2,1,0,3:T(8,128)}, u32[]{:S(2)}, u32[]{:S(2)}) async-start(f32[2,8,128,2048]{2,1,0,3:T(8,128)} %copy.199), calls=%async_computation.3 | async-start | bytes 33554432 | tf_op jit(solution)/shard_map/all_to_all | solution.py:71
  1578.1 105.9 %copy-start = (f32[1,256,4,16,128]{4,1,3,2,0:T(8,128)}, f32[1,256,4,16,128]{4,1,3,2,0:T(8,128)S(1)}, u32[]{:S(2)}) copy-start(f32[1,256,4,16,128]{4,1,3,2,0:T(8,128)S(1)} %copy.219) | copy-start | bytes 25165828
  1578.1 9.0 copy-start.6
  1587.1 86.0 %copy-start.1 = (f32[1,256,4,16,128]{4,1,3,2,0:T(8,128)}, f32[1,256,4,16,128]{4,1,3,2,0:T(8,128)S(1)}, u32[]{:S(2)}) copy-start(f32[1,256,4,16,128]{4,1,3,2,0:T(8,128)S(1)} %copy.220) | copy-start | bytes 25165828
  1638.8 17.1 copy-start.4
  1711.7 18.4 copy-start.9
  1711.7 18.4 copy-start.15
  1764.0 455.8 %all-to-all-start.5 = ((f32[2,256,64,128]{3,1,0,2:T(8,128)}), f32[2,256,64,128]{3,1,0,2:T(8,128)}, u32[]{:S(2)}, u32[]{:S(2)}) async-start(f32[2,256,64,128]{3,1,0,2:T(8,128)} %copy.231), calls=%async_computation.5 | async-start | bytes 33554432 | tf_op jit(solution)/shard_map/all_to_all | solution.py:78
  1871.6 7.8 copy-start.2
  1987.2 18.7 slice-start.2
  1987.2 27.8 %slice-start = ((s8[8388608]{0:T(1024)(128)(4,1)}), s8[4194304]{0:T(1024)(128)(4,1)S(1)}, s32[]{:S(2)}) async-start(s8[8388608]{0:T(1024)(128)(4,1)} %bitcast.271), calls=%async_computation.6 | async-start | bytes 8388608
  1996.5 9.4 slice-start.3
  1996.5 18.5 slice-start.1
  2035.5 11.3 copy-start.10
  2035.5 11.3 copy-start.13
  2219.7 190.7 %all-to-all-start.4 = ((f32[2,64,128,256]{2,3,0,1:T(8,128)}), f32[2,64,128,256]{2,3,0,1:T(8,128)}, u32[]{:S(2)}, u32[]{:S(2)}) async-start(f32[2,64,128,256]{2,3,0,1:T(8,128)} %copy.213), calls=%async_computation.4 | async-start | bytes 33554432 | tf_op jit(solution)/shard_map/all_to_all | solution.py:73
